TPU v7x, 512 devices: a whole 4x8x8 slice. The times are simulated.
512 devices in a mesh: facet: 64 (over y_hi, z, x), band: 8 (over y_lo, core).
Axes of the slice: x: 4, y: 8 (y_hi: 2, y_lo: 4; y = y_hi * 4 + y_lo), z: 8, core: 2. Of those that a mesh axis runs over, the one named last changes fastest.
Arguments:
- facet_strips: float32 [8, 64, 2, 8, 4096], P('band', 'facet'), may hold values from -6 to 6
- subgrid_offsets: int32 [2, 64], replicated, may hold values from 0 to 4095
- sample_cells: int32 [8, 2, 64, 2, 512], P('band', None, 'facet'), may hold values from 0 to 511, as said below
- sample_values: float32 [8, 2, 64, 2, 512], P('band', None, 'facet'), may hold values from -6 to 6
- sample_weights: float32 [8, 2, 64, 512], P('band', None, 'facet'), may hold values from 0.1 to 1
- sample_flags: int32 [8, 2, 64, 512], P('band', None, 'facet'), may hold values 0 or 1
Outputs:
- residual_strips: float32 [64, 8, 2, 4096], P('facet', 'band')
Inputs may be any that keep to these rules, and one draw needn't show every extreme that they name: `sample_cells`: slot 0 holds a row of 0 to (64 // 8) * 8 - 1, slot 1 a column of 0 to 512 - 1; every subgrid of every sub-band and front has a sample at its last row and last column.
All inputs are finite; a program needn't handle non-finite values. No bound on the sum of `sample_flags` on one device may be relied on, other than what follows from the above.
Results may differ from a plain program's by a relative error of at most 0.006.
Values may be sent and summed in bfloat16 or wider, within the bound.
A program may use at most 64 MiB of HBM per device.

v0:
```python
import math

import jax
import jax.numpy as jnp
import numpy as np
from jax import lax
from jax.experimental import pallas as pl
from jax.experimental.pallas import tpu as pltpu
from jax.sharding import PartitionSpec as P

FN = 4096
CONTRIB = 64
FACET_ROWS = 8
COLS = 8
FRONTS = 2
SG = 512
VIS = 512
EXACT = lax.Precision.HIGHEST


def unit_table(length, rotation, rows, cols):
    angle = np.outer(np.arange(rows), np.arange(cols)) % length * (2.0 * np.pi / length)
    return np.cos(angle), rotation * np.sin(angle)


def real_form(cosine, sine):
    return np.block([[cosine, sine], [-sine, cosine]])


def f32(x):
    return jnp.asarray(np.asarray(x, np.float32))


def phase_table():
    cosine, sine = unit_table(SG, -1.0, CONTRIB, SG)
    cos8, sin8 = unit_table(8, -1.0, 8, SG)
    table = np.concatenate([cosine, sine, cos8, sin8], axis=0).astype(np.float32)
    high = table.astype(jnp.bfloat16)
    low = (table - high.astype(np.float32)).astype(jnp.bfloat16)
    return jnp.asarray(np.stack([high, low]))


def phase_kernel(table_ref, cells_ref, out_ref):
    for t in range(FRONTS):
        col = cells_ref[t, 1:2, :]
        hot = (lax.broadcasted_iota(jnp.int32, (SG, VIS), 0) == col).astype(jnp.float32)
        hot = hot.astype(jnp.bfloat16)
        out_ref[t] = jnp.dot(
            table_ref[0], hot, preferred_element_type=jnp.float32
        ) + jnp.dot(table_ref[1], hot, preferred_element_type=jnp.float32)


def subgrid_kernel(
    image_ref, phase_ref, cells_ref, values_ref, weights_ref, flags_ref, out_ref
):
    scale = SG ** (-0.5)
    half = CONTRIB
    for t in range(FRONTS):
        row = cells_ref[t, 0:1, :]
        place = lax.broadcasted_iota(jnp.int32, (COLS * 8, VIS), 0)
        hot = (place == row).astype(jnp.float32).astype(jnp.bfloat16)
        turned = (row & 7) * 8 + (row >> 3)
        hot_back = (place == turned).astype(jnp.float32).astype(jnp.bfloat16)
        er = phase_ref[t, 0:half, :]
        ei = phase_ref[t, half : 2 * half, :]
        pred_re = jnp.zeros((1, VIS), jnp.float32)
        pred_im = jnp.zeros((1, VIS), jnp.float32)
        for i in range(FACET_ROWS):
            slab = image_ref[:, i, t].astype(jnp.float32).reshape(COLS * 8, 2 * half)
            slab = slab.astype(jnp.bfloat16)
            picked = lax.dot_general(
                slab, hot, (((0,), (0,)), ((), ())), preferred_element_type=jnp.float32
            )
            pr = picked[:half]
            pi = picked[half:]
            sr = jnp.sum(pr * er - pi * ei, axis=0, keepdims=True)
            si = jnp.sum(pr * ei + pi * er, axis=0, keepdims=True)
            c8 = phase_ref[t, 2 * half + i : 2 * half + i + 1, :]
            s8 = phase_ref[t, 2 * half + 8 + i : 2 * half + 9 + i, :]
            pred_re += c8 * sr - s8 * si
            pred_im += c8 * si + s8 * sr
        factor = weights_ref[t : t + 1, :] * flags_ref[t : t + 1, :].astype(jnp.float32)
        res_re = factor * (values_ref[t, 0:1, :] - scale * pred_re) * scale
        res_im = factor * (values_ref[t, 1:2, :] - scale * pred_im) * scale
        for i in range(FACET_ROWS):
            c8 = phase_ref[t, 2 * half + i : 2 * half + i + 1, :]
            s8 = phase_ref[t, 2 * half + 8 + i : 2 * half + 9 + i, :]
            gr = res_re * c8 + res_im * s8
            gi = res_im * c8 - res_re * s8
            wave = jnp.concatenate([gr * er + gi * ei, gi * er - gr * ei], axis=0)
            back = lax.dot_general(
                hot_back,
                wave.astype(jnp.bfloat16),
                (((1,), (1,)), ((), ())),
                preferred_element_type=jnp.float32,
            )
            out_ref[:, t, 8 * i : 8 * i + 8, :] = back.reshape(COLS, 8, 2 * half).astype(
                jnp.bfloat16
            )


def local(facet_strips, subgrid_offsets, sample_cells, sample_values, sample_weights, sample_flags):
    vmem = pl.BlockSpec(memory_space=pltpu.VMEM)
    facets = lax.axis_size("facet")
    windows = facets * FRONTS
    blocks = FN // CONTRIB
    n = np.arange(FN)
    window = (1.0 + 0.5 * np.cos(2.0 * np.pi * n / FN)) * FN ** (-0.5)
    offsets = jnp.transpose(subgrid_offsets).reshape(windows)
    first = offsets // CONTRIB
    shift = offsets % CONTRIB
    block_index = lax.iota(jnp.int32, blocks)
    pick = jnp.concatenate([first, (first + 1) % blocks])[:, None] == block_index[None, :]
    pick = pick.astype(jnp.float32)
    inside = lax.iota(jnp.int32, CONTRIB)[None, :] >= shift[:, None]
    angle = (shift[:, None] * lax.iota(jnp.int32, CONTRIB)[None, :] % CONTRIB).astype(
        jnp.float32
    ) * (2.0 * math.pi / CONTRIB)
    ramp_cos = jnp.cos(angle)
    ramp_sin = jnp.sin(angle)

    short = real_form(*unit_table(CONTRIB, -1.0, CONTRIB, CONTRIB)).reshape(2, 64, 2, 64)
    turn_cos, turn_sin = unit_table(FN, 1.0, CONTRIB, CONTRIB)
    strips = (facet_strips[0, 0] * f32(window)).reshape(2, COLS, CONTRIB, CONTRIB)
    section = jnp.einsum("rcan,rasp->scpn", strips, f32(short), precision=EXACT)
    tc, ts = f32(turn_cos), f32(turn_sin)
    turned = jnp.stack(
        [section[0] * tc + section[1] * ts, section[1] * tc - section[0] * ts], axis=0
    )
    spectrum = jnp.einsum("rcpn,rnsb->bcsp", turned, f32(short), precision=EXACT)
    chosen = jnp.dot(pick, spectrum.reshape(blocks, -1), precision=EXACT)
    chosen = chosen.reshape(2, windows, COLS * 2, CONTRIB)
    cut = jnp.where(inside[:, None, :], chosen[0], chosen[1]).reshape(windows * COLS, 128)
    plus = real_form(*unit_table(CONTRIB, 1.0, CONTRIB, CONTRIB)) * CONTRIB ** (-0.5)
    plus = np.concatenate([plus, plus[:, 64:], plus[:, :64]], axis=1)
    piece = jnp.dot(cut, f32(plus), precision=lax.Precision.HIGH).reshape(windows, COLS, 256)
    ramp_c = jnp.concatenate([ramp_cos, ramp_cos], axis=1)
    ramp_s = jnp.concatenate([ramp_sin, -ramp_sin], axis=1)
    piece = piece[..., :128] * ramp_c[:, None] + piece[..., 128:] * ramp_s[:, None]
    leaving = piece.astype(jnp.bfloat16).reshape(facets, FRONTS, COLS, 128)
    arrived = lax.all_to_all(leaving, "facet", split_axis=0, concat_axis=0, tiled=True)

    cells = sample_cells.reshape(FRONTS, 2, VIS)
    phases = pl.pallas_call(
        phase_kernel,
        out_shape=jax.ShapeDtypeStruct((FRONTS, 144, VIS), jnp.float32),
        in_specs=[vmem] * 2,
        out_specs=vmem,
        cost_estimate=pl.CostEstimate(
            flops=4 * 144 * SG * VIS * 2, bytes_accessed=1 << 20, transcendentals=0
        ),
    )(phase_table(), cells)
    returned = pl.pallas_call(
        subgrid_kernel,
        out_shape=jax.ShapeDtypeStruct((COLS, FRONTS, facets, 128), jnp.bfloat16),
        in_specs=[vmem] * 6,
        out_specs=vmem,
    )(
        arrived.reshape(facets // FACET_ROWS, FACET_ROWS, FRONTS, COLS, 128),
        phases,
        cells,
        sample_values.reshape(FRONTS, 2, VIS),
        sample_weights.reshape(FRONTS, VIS),
        sample_flags.reshape(FRONTS, VIS),
    )

    banded = lax.all_to_all(returned, "band", split_axis=0, concat_axis=0, tiled=True)
    summed = jnp.sum(banded.astype(jnp.float32), axis=0)
    summed = summed.reshape(FRONTS, FACET_ROWS, facets // FACET_ROWS, 128)
    summed = jnp.transpose(summed, (2, 1, 0, 3)).reshape(facets, FRONTS, 128)
    delivered = lax.all_to_all(
        summed.astype(jnp.bfloat16), "facet", split_axis=0, concat_axis=0, tiled=True
    )
    delivered = delivered.astype(jnp.float32).reshape(windows, 2, CONTRIB)
    dr, di = delivered[:, 0], delivered[:, 1]
    aligned = jnp.concatenate(
        [dr * ramp_cos - di * ramp_sin, di * ramp_cos + dr * ramp_sin], axis=1
    )
    minus = short.reshape(128, 128) * CONTRIB ** (-0.5)
    partial = jnp.dot(aligned, f32(minus), precision=EXACT)
    inside2 = jnp.concatenate([inside, inside], axis=1)
    masked = jnp.concatenate(
        [jnp.where(inside2, partial, 0.0), jnp.where(inside2, 0.0, partial)], axis=0
    )
    spread = lax.dot_general(pick, masked, (((0,), (0,)), ((), ())), precision=EXACT)
    spread = spread.reshape(blocks, 2, CONTRIB)
    plus4 = real_form(*unit_table(CONTRIB, 1.0, CONTRIB, CONTRIB)).reshape(2, 64, 2, 64)
    line = jnp.einsum("brp,rbsn->spn", spread, f32(plus4), precision=EXACT)
    line = jnp.stack([line[0] * tc - line[1] * ts, line[1] * tc + line[0] * ts], axis=0)
    line = jnp.einsum("rpn,rpsa->san", line, f32(plus4), precision=EXACT)
    result = line.reshape(2, FN) * f32(window)
    return result[None, None]


def solution(mesh):
    placed = (
        P("band", "facet", None, None, None),
        P(),
        P("band", None, "facet", None, None),
        P("band", None, "facet", None, None),
        P("band", None, "facet", None),
        P("band", None, "facet", None),
    )
    return jax.shard_map(
        local, mesh=mesh, in_specs=placed, out_specs=P("facet", "band", None, None), check_vma=False
    )
```

profile of v0, /device:TPU:1, one launch (start us, length us, event | category | flops | bytes accessed | tf_op | source)
XLA Modules:
  0.0 86.1 jit_solution(16958397763741556695)
XLA Ops:
  0.0 0.7 copy-done.13
  0.7 0.1 copy.53
  0.8 0.1 reshape.134
  0.9 0.1 iota_compare_fusion.3
  1.0 0.3 fusion.33
  1.4 0.2 squeeze.27
  1.6 0.2 copy.55
  1.9 0.7 copy-done.1
  2.5 0.6 convolution_bitcast_fusion
  3.1 0.1 copy-done.6
  3.3 0.0 copy-done.7
  3.3 0.1 multiply_add_fusion
  3.4 1.1 %fusion.2 = f32[8,64,2,64,1]{3,1,4,2,0:T(8,128)S(1)} fusion(f32[2,64,2,64,1]{3,1,0,2,4:T(8,128)S(1)} %copy-done.1, f32[1,8,64,64]{2,3,0,1:T(8,128)S(1)} %get-tuple-element.10, f32[1,8,64,64]{2,3,0,1:T(8,128)S(1)} %get-tuple-element.9), kind=kOutput, calls=%fused_computation.9 | convolution fusion | flops 100728832 | bytes 589824 | tf_op jit(solution)/shard_map/rcpn,rnsb->bcsp/dot_general | solution.py:130
  4.4 0.6 fusion.14
  5.1 0.1 fusion.51
  5.1 0.2 copy.77
  5.3 0.2 copy.78
  5.5 0.1 copy.54
  5.6 0.1 pad_maximum_fusion
  5.8 0.9 copy-done.4
  6.6 0.6 fusion.6
  7.3 0.1 fusion.1
  7.4 1.0 %copy.60 = bf16[64,2,8,128]{3,2,1,0:T(8,128)(2,1)} copy(bf16[64,2,8,128]{3,1,0,2:T(2,128)(2,1)S(1)} %bitcast.78) | data formatting | bytes 524288 | tf_op jit(solution)/shard_map/reshape | solution.py:140
  8.4 19.7 %all-to-all-start = ((bf16[64,2,8,128]{3,2,1,0:T(8,128)(2,1)}), bf16[64,2,8,128]{3,2,1,0:T(8,128)(2,1)S(1)}, u32[]{:S(2)}, u32[]{:S(2)}) async-start(bf16[64,2,8,128]{3,2,1,0:T(8,128)(2,1)} %copy.60), calls=%async_computation | async-start | bytes 524288 | tf_op jit(solution)/shard_map/all_to_all | solution.py:141
  28.1 0.6 copy.88
  28.7 0.1 copy-done.12
  28.8 0.6 copy.89
  29.4 2.4 %shard_map.163.phase_ref = f32[2,144,512]{2,1,0:T(8,128)} custom-call(bf16[2,144,512]{2,1,0:T(8,128)(2,1)} %constant.69.clone.table_ref, s32[2,2,512]{2,1,0:T(2,128)} %bitcast.89), custom_call_target="tpu_custom_call" | custom-call | flops 301989888 | bytes 1048576 | tf_op jit(solution)/shard_map/pallas_call | solution.py:144
  31.8 10.3 %all-to-all-done = bf16[64,2,8,128]{3,2,1,0:T(8,128)(2,1)S(1)} async-done(((bf16[64,2,8,128]{3,2,1,0:T(8,128)(2,1)}), bf16[64,2,8,128]{3,2,1,0:T(8,128)(2,1)S(1)}, u32[]{:S(2)}, u32[]{:S(2)}) %all-to-all-start) | async-done | bytes 262176 | tf_op jit(solution)/shard_map/all_to_all | solution.py:141
  42.1 0.7 copy-done
  42.8 4.0 %shard_map.164 = bf16[8,2,64,128]{3,2,1,0:T(8,128)(2,1)} custom-call(bf16[8,8,2,8,128]{4,3,2,1,0:T(8,128)(2,1)} %bitcast.77, f32[2,144,512]{2,1,0:T(8,128)} %shard_map.163.phase_ref, s32[2,2,512]{2,1,0:T(2,128)} %bitcast.90, f32[2,2,512]{2,1,0:T(2,128)} %bitcast.91, f32[2,512]{1,0:T(2,128)} %bitcast.88, s32[2,512]{1,0:T(2,128)} %bitcast.87), custom_call_target="tpu_custom_call" | custom-call | tf_op jit(solution)/shard_map/pallas_call | solution.py:153
  46.8 15.5 %all_to_all.15 = bf16[8,2,64,128]{3,2,1,0:T(8,128)(2,1)S(1)} all-to-all(bf16[8,2,64,128]{3,2,1,0:T(8,128)(2,1)} %shard_map.164), channel_id=1, replica_groups=mesh['facet'=64,'band'=8] {'band'}, dimensions={0} | all-to-all | bytes 524288 | tf_op jit(solution)/shard_map/all_to_all | solution.py:167
  62.4 18.1 %all_to_all.16 = bf16[64,2,128]{2,1,0:T(2,128)(2,1)S(1)} all-to-all(bf16[64,2,128]{2,1,0:T(2,128)(2,1)S(1)} %copy.62), channel_id=1, replica_groups=mesh['facet'=64,'band'=8] {'facet'}, dimensions={0} | all-to-all | bytes 65536 | tf_op jit(solution)/shard_map/all_to_all | solution.py:171
  80.5 0.1 reshape.147
  80.7 0.1 fusion.52
  80.8 0.6 copy-done.15
  81.4 0.5 fusion.23
  81.9 0.2 copy-done.14
  82.2 0.5 broadcast_select_fusion.1
  82.7 0.3 fusion.10
  83.1 0.6 copy-done.2
  83.6 0.3 convolution_bitcast_fusion.2
  83.9 0.5 copy-done.8
  84.4 0.0 copy-done.9
  84.4 0.4 convolution_bitcast_fusion.1
  84.8 0.1 reshape.145
  84.9 0.6 copy-done.10
  85.5 0.6 broadcast_multiply_fusion
  (26 shorter events, 0.2 us)
Async XLA Ops:
  0.0 0.7 copy-start.13
  0.0 1.4 %copy-start.3 = (f32[1,1,2,8,4096]{4,3,2,1,0:T(8,128)S(1)}, f32[1,1,2,8,4096]{4,3,2,1,0:T(8,128)}, u32[]{:S(2)}) copy-start(f32[1,1,2,8,4096]{4,3,2,1,0:T(8,128)} %param.17) | copy-start | bytes 786436
  1.6 0.9 %copy-start.1 = (f32[2,64,2,64,1]{3,1,0,2,4:T(8,128)S(1)}, f32[2,64,2,64,1]{3,1,0,2,4:T(8,128)}, u32[]{:S(2)}) copy-start(f32[2,64,2,64,1]{3,1,0,2,4:T(8,128)} %constant.84) | copy-start | bytes 196612
  1.6 0.9 %copy-start.5 = (f32[64,64]{0,1:T(8,128)S(1)}, f32[64,64]{0,1:T(8,128)}, u32[]{:S(2)}) copy-start(f32[64,64]{0,1:T(8,128)} %constant.77) | copy-start | bytes 49156
  2.5 0.8 copy-start.6
  2.5 0.8 copy-start.7
  5.7 0.9 %copy-start.4 = (f32[128,256,1]{1,0,2:T(8,128)S(1)}, f32[128,256,1]{1,0,2:T(8,128)}, u32[]{:S(2)}) copy-start(f32[128,256,1]{1,0,2:T(8,128)} %constant.85) | copy-start | bytes 393220
  8.4 19.7 %copy-start.11 = (s32[1,2,1,512]{3,2,1,0:T(1,128)S(1)}, s32[1,2,1,512]{3,2,1,0:T(1,128)}, u32[]{:S(2)}) copy-start(s32[1,2,1,512]{3,2,1,0:T(1,128)} %param.22) | copy-start | bytes 12292
  8.4 33.7 %all-to-all-start = ((bf16[64,2,8,128]{3,2,1,0:T(8,128)(2,1)}), bf16[64,2,8,128]{3,2,1,0:T(8,128)(2,1)S(1)}, u32[]{:S(2)}, u32[]{:S(2)}) async-start(bf16[64,2,8,128]{3,2,1,0:T(8,128)(2,1)} %copy.60), calls=%async_computation | async-start | bytes 524288 | tf_op jit(solution)/shard_map/all_to_all | solution.py:141
  28.1 0.7 copy-start.12
  42.1 0.7 copy-start
  80.6 0.8 copy-start.15
  81.4 0.8 copy-start.14
  82.7 0.9 %copy-start.2 = (f32[2,64,2,64]{3,1,0,2:T(8,128)S(1)}, f32[2,64,2,64]{3,1,0,2:T(8,128)}, u32[]{:S(2)}) copy-start(f32[2,64,2,64]{3,1,0,2:T(8,128)} %constant.71.clone) | copy-start | bytes 196612
  83.6 0.8 copy-start.8
  83.6 0.8 copy-start.9
  84.8 0.7 copy-start.10
where the time goes:
time: 87 us; the launch traced here: 86.1 us
  blocking collectives  33.6 us (39%)
  starting transfers between devices  19.7 us (23%)
  waiting for transfers between devices  10.3 us (12%)
  local copies, waits for them, and re-layouts  9.51 us (11%)
  Pallas kernels  6.41 us (7%)
  matrix products  4.92 us (6%)
  other arithmetic  1.38 us (2%)
    all_to_all x1, starting transfers between devices, local(): lax.all_to_all(leaving, 'facet', split_axis=0, concat_axis=0, tiled=True)  19.7 us
    all_to_all x1, blocking collectives, local(): lax.all_to_all(summed.astype(jnp.bfloat16), 'facet', split_axis=0, concat...  18.1 us
    all_to_all x1, blocking collectives, local(): lax.all_to_all(returned, 'band', split_axis=0, concat_axis=0, tiled=True)  15.5 us
    all_to_all x1, waiting for transfers between devices, local(): lax.all_to_all(leaving, 'facet', split_axis=0, concat_axis=0, tiled=True)  10.3 us
    unnamed x34, local copies, waits for them, and re-layouts  6.9 us
    pallas_call x1, Pallas kernels, local(): pl.pallas_call(subgrid_kernel, out_shape=jax.ShapeDtypeStruct((COLS, FRON...  4.04 us
    pallas_call x1, Pallas kernels, local(): pl.pallas_call(phase_kernel, out_shape=jax.ShapeDtypeStruct((FRONTS, 144,...  2.37 us
  transfers between devices with their start and end apart: 1, of which 1 were waited for; matrix products, arithmetic and copies ran while one was open for 1% of the time, Pallas kernels for 3%

commit v1 on v0

--- a/solution.py
+++ b/solution.py
@@ -40,34 +40,96 @@
     return jnp.asarray(np.stack([high, low]))
 
 
-def phase_kernel(table_ref, cells_ref, out_ref):
+def exchange_kernel(
+    leaving_ref,
+    table_ref,
+    cells_ref,
+    values_ref,
+    weights_ref,
+    flags_ref,
+    out_ref,
+    arrived_ref,
+    phase_ref,
+    back_ref,
+    banded_ref,
+    sum_ref,
+    landed_ref,
+    sems,
+):
+    facets = leaving_ref.shape[0]
+    bands = back_ref.shape[0]
+    groups = facets // FACET_ROWS
+    me = lax.axis_index("facet")
+    band = lax.axis_index("band")
+
+    barrier = pltpu.get_barrier_semaphore()
+
+    @pl.loop(1, facets)
+    def _(k):
+        pl.semaphore_signal(
+            barrier, inc=1, device_id={"facet": lax.rem(me + k, facets)},
+            device_id_type=pl.DeviceIdType.MESH,
+        )
+
+    @pl.loop(1, bands)
+    def _(k):
+        pl.semaphore_signal(
+            barrier, inc=1, device_id={"band": lax.rem(band + k, bands)},
+            device_id_type=pl.DeviceIdType.MESH,
+        )
+
+    pl.semaphore_wait(barrier, facets + bands - 2)
+
+    def whole(ref, count, sem):
+        part = ref.at[pl.ds(0, count)]
+        pltpu.make_async_copy(part, part, sem).wait()
+
+    own = pltpu.make_async_copy(leaving_ref.at[me], arrived_ref.at[me], sems.at[2])
+    own.start()
+
+    @pl.loop(1, facets)
+    def _(k):
+        to = lax.rem(me + 27 * k, facets)
+        pltpu.make_async_remote_copy(
+            src_ref=leaving_ref.at[to],
+            dst_ref=arrived_ref.at[me],
+            send_sem=sems.at[0],
+            recv_sem=sems.at[1],
+            device_id={"facet": to},
+            device_id_type=pl.DeviceIdType.MESH,
+        ).start()
+
     for t in range(FRONTS):
         col = cells_ref[t, 1:2, :]
         hot = (lax.broadcasted_iota(jnp.int32, (SG, VIS), 0) == col).astype(jnp.float32)
         hot = hot.astype(jnp.bfloat16)
-        out_ref[t] = jnp.dot(
+        phase_ref[t] = jnp.dot(
             table_ref[0], hot, preferred_element_type=jnp.float32
         ) + jnp.dot(table_ref[1], hot, preferred_element_type=jnp.float32)
-
-
-def subgrid_kernel(
-    image_ref, phase_ref, cells_ref, values_ref, weights_ref, flags_ref, out_ref
-):
+    own.wait()
+    whole(leaving_ref, facets - 1, sems.at[0])
+    whole(arrived_ref, facets - 1, sems.at[1])
+
     scale = SG ** (-0.5)
     half = CONTRIB
     for t in range(FRONTS):
         row = cells_ref[t, 0:1, :]
-        place = lax.broadcasted_iota(jnp.int32, (COLS * 8, VIS), 0)
+        place = lax.broadcasted_iota(jnp.int32, (COLS * groups, VIS), 0)
         hot = (place == row).astype(jnp.float32).astype(jnp.bfloat16)
-        turned = (row & 7) * 8 + (row >> 3)
+        turned = (row & 7) * groups + (row >> 3)
         hot_back = (place == turned).astype(jnp.float32).astype(jnp.bfloat16)
         er = phase_ref[t, 0:half, :]
         ei = phase_ref[t, half : 2 * half, :]
         pred_re = jnp.zeros((1, VIS), jnp.float32)
         pred_im = jnp.zeros((1, VIS), jnp.float32)
         for i in range(FACET_ROWS):
-            slab = image_ref[:, i, t].astype(jnp.float32).reshape(COLS * 8, 2 * half)
-            slab = slab.astype(jnp.bfloat16)
+            slab = jnp.concatenate(
+                [
+                    arrived_ref[FACET_ROWS * j + i, t].astype(jnp.float32)
+                    for j in range(groups)
+                ],
+                axis=0,
+            ).astype(jnp.bfloat16)
             picked = lax.dot_general(
                 slab, hot, (((0,), (0,)), ((), ())), preferred_element_type=jnp.float32
             )
@@ -94,9 +156,55 @@
                 (((1,), (1,)), ((), ())),
                 preferred_element_type=jnp.float32,
             )
-            out_ref[:, t, 8 * i : 8 * i + 8, :] = back.reshape(COLS, 8, 2 * half).astype(
-                jnp.bfloat16
-            )
+            back_ref[:, t, groups * i : groups * (i + 1), :] = back.reshape(
+                COLS, groups, 2 * half
+            ).astype(jnp.bfloat16)
+
+    own = pltpu.make_async_copy(back_ref.at[band], banded_ref.at[band], sems.at[5])
+    own.start()
+
+    @pl.loop(1, bands)
+    def _(k):
+        to = lax.rem(band + k, bands)
+        pltpu.make_async_remote_copy(
+            src_ref=back_ref.at[to],
+            dst_ref=banded_ref.at[band],
+            send_sem=sems.at[3],
+            recv_sem=sems.at[4],
+            device_id={"band": to},
+            device_id_type=pl.DeviceIdType.MESH,
+        ).start()
+
+    own.wait()
+    whole(back_ref, bands - 1, sems.at[3])
+    whole(banded_ref, bands - 1, sems.at[4])
+    for t in range(FRONTS):
+        total = banded_ref[0, t].astype(jnp.float32)
+        for b in range(1, bands):
+            total += banded_ref[b, t].astype(jnp.float32)
+        sum_ref[:, t, :] = total
+
+    mine = lax.rem(me, FACET_ROWS) * groups + me // FACET_ROWS
+    own = pltpu.make_async_copy(sum_ref.at[mine], landed_ref.at[me], sems.at[8])
+    own.start()
+
+    @pl.loop(1, facets)
+    def _(k):
+        to = lax.rem(me + 27 * k, facets)
+        slot = lax.rem(to, FACET_ROWS) * groups + to // FACET_ROWS
+        pltpu.make_async_remote_copy(
+            src_ref=sum_ref.at[slot],
+            dst_ref=landed_ref.at[me],
+            send_sem=sems.at[6],
+            recv_sem=sems.at[7],
+            device_id={"facet": to},
+            device_id_type=pl.DeviceIdType.MESH,
+        ).start()
+
+    own.wait()
+    whole(sum_ref, facets - 1, sems.at[6])
+    whole(landed_ref, facets - 1, sems.at[7])
+    out_ref[...] = landed_ref[...]
 
 
 def local(facet_strips, subgrid_offsets, sample_cells, sample_values, sample_weights, sample_flags):
@@ -138,40 +246,32 @@
     ramp_s = jnp.concatenate([ramp_sin, -ramp_sin], axis=1)
     piece = piece[..., :128] * ramp_c[:, None] + piece[..., 128:] * ramp_s[:, None]
     leaving = piece.astype(jnp.bfloat16).reshape(facets, FRONTS, COLS, 128)
-    arrived = lax.all_to_all(leaving, "facet", split_axis=0, concat_axis=0, tiled=True)
-
-    cells = sample_cells.reshape(FRONTS, 2, VIS)
-    phases = pl.pallas_call(
-        phase_kernel,
-        out_shape=jax.ShapeDtypeStruct((FRONTS, 144, VIS), jnp.float32),
-        in_specs=[vmem] * 2,
-        out_specs=vmem,
-        cost_estimate=pl.CostEstimate(
-            flops=4 * 144 * SG * VIS * 2, bytes_accessed=1 << 20, transcendentals=0
-        ),
-    )(phase_table(), cells)
-    returned = pl.pallas_call(
-        subgrid_kernel,
-        out_shape=jax.ShapeDtypeStruct((COLS, FRONTS, facets, 128), jnp.bfloat16),
+
+    bands = lax.axis_size("band")
+    delivered = pl.pallas_call(
+        exchange_kernel,
+        out_shape=jax.ShapeDtypeStruct((facets, FRONTS, 128), jnp.float32),
         in_specs=[vmem] * 6,
         out_specs=vmem,
+        scratch_shapes=[
+            pltpu.VMEM((facets, FRONTS, COLS, 128), jnp.bfloat16),
+            pltpu.VMEM((FRONTS, 144, VIS), jnp.float32),
+            pltpu.VMEM((bands, FRONTS, facets, 128), jnp.bfloat16),
+            pltpu.VMEM((bands, FRONTS, facets, 128), jnp.bfloat16),
+            pltpu.VMEM((facets, FRONTS, 128), jnp.float32),
+            pltpu.VMEM((facets, FRONTS, 128), jnp.float32),
+            pltpu.SemaphoreType.DMA((9,)),
+        ],
+        compiler_params=pltpu.CompilerParams(collective_id=0, has_side_effects=True),
     )(
-        arrived.reshape(facets // FACET_ROWS, FACET_ROWS, FRONTS, COLS, 128),
-        phases,
-        cells,
+        leaving,
+        phase_table(),
+        sample_cells.reshape(FRONTS, 2, VIS),
         sample_values.reshape(FRONTS, 2, VIS),
         sample_weights.reshape(FRONTS, VIS),
         sample_flags.reshape(FRONTS, VIS),
     )
-
-    banded = lax.all_to_all(returned, "band", split_axis=0, concat_axis=0, tiled=True)
-    summed = jnp.sum(banded.astype(jnp.float32), axis=0)
-    summed = summed.reshape(FRONTS, FACET_ROWS, facets // FACET_ROWS, 128)
-    summed = jnp.transpose(summed, (2, 1, 0, 3)).reshape(facets, FRONTS, 128)
-    delivered = lax.all_to_all(
-        summed.astype(jnp.bfloat16), "facet", split_axis=0, concat_axis=0, tiled=True
-    )
-    delivered = delivered.astype(jnp.float32).reshape(windows, 2, CONTRIB)
+    delivered = delivered.reshape(windows, 2, CONTRIB)
     dr, di = delivered[:, 0], delivered[:, 1]
     aligned = jnp.concatenate(
         [dr * ramp_cos - di * ramp_sin, di * ramp_cos + dr * ramp_sin], axis=1

time: 87 us -> 65.3 us (0.75)
  Pallas kernels: 6.41 us -> 47.9 us
  blocking collectives: 33.6 us -> 0 us
  starting transfers between devices: 19.7 us -> 0 us
  waiting for transfers between devices: 10.3 us -> 0 us
    pallas_call x2 -> x1, Pallas kernels: 6.41 us -> 47.9 us  [local(): pl.pallas_call(exchange_kernel, out_shape=jax.ShapeDtypeStruct((facets, F...]
    all_to_all x2 -> x0, blocking collectives: 33.6 us -> none  [the longest x1 18.1 us: local(): lax.all_to_all(summed.astype(jnp.bfloat16), 'facet', split_axis=0, concat...]
    all_to_all x1 -> x0, starting transfers between devices: 19.7 us -> none  [local(): lax.all_to_all(leaving, 'facet', split_axis=0, concat_axis=0, tiled=True)]
    all_to_all x1 -> x0, waiting for transfers between devices: 10.3 us -> none  [local(): lax.all_to_all(leaving, 'facet', split_axis=0, concat_axis=0, tiled=True)]
    squeeze x2, local copies, waits for them, and re-layouts: 0.41 us -> 1.34 us  [local(): facet_strips[0, 0] * f32(window)]
    unnamed x34 -> x30, local copies, waits for them, and re-layouts: 6.9 us -> 6.04 us
  transfers between devices with their start and end apart: 1 -> 0, of which waited for: 1 -> 0; matrix products, arithmetic and copies ran while one was open for 1% -> 0% of each run, Pallas kernels for 3% -> 0%
where the time goes in v1:
time: 65.3 us; the launch traced here: 64.7 us
  Pallas kernels  47.9 us (73%)
  local copies, waits for them, and re-layouts  10.2 us (16%)
  matrix products  4.92 us (8%)
  other arithmetic  1.34 us (2%)
    pallas_call x1, Pallas kernels, local(): pl.pallas_call(exchange_kernel, out_shape=jax.ShapeDtypeStruct((facets, F...  47.9 us
    unnamed x30, local copies, waits for them, and re-layouts  6.04 us
    squeeze x2, local copies, waits for them, and re-layouts, local(): facet_strips[0, 0] * f32(window)  1.34 us

profile of v1, /device:TPU:1, one launch (start us, length us, event | category | flops | bytes accessed | tf_op | source)
XLA Modules:
  0.0 64.7 jit_solution(859157796078502896)
XLA Ops:
  0.0 0.7 %copy-done.11 = s32[2,64]{1,0:T(2,128)S(1)} copy-done((s32[2,64]{1,0:T(2,128)S(1)}, s32[2,64]{1,0:T(2,128)}, u32[]{:S(2)}) %copy-start.11) | copy-done | bytes 536
  0.7 0.1 copy.28
  0.8 0.1 reshape.124
  1.0 1.1 %squeeze.27 = f32[2,8,64,64]{3,2,1,0:T(8,128)S(1)} reshape(f32[1,1,2,8,4096]{4,3,2,1,0:T(8,128)} %param.17) | data formatting | bytes 524288 | tf_op jit(solution)/shard_map/squeeze | solution.py:232
  2.1 0.0 copy-start
  2.1 0.0 copy-start.3
  2.1 0.2 copy.30
  2.3 0.7 %copy-done = f32[2,64,2,64,1]{3,1,0,2,4:T(8,128)S(1)} copy-done((f32[2,64,2,64,1]{3,1,0,2,4:T(8,128)S(1)}, f32[2,64,2,64,1]{3,1,0,2,4:T(8,128)}, u32[]{:S(2)}) %copy-start) | copy-done | bytes 65560
  3.0 0.6 convolution_bitcast_fusion
  3.6 0.1 copy-done.4
  3.8 0.0 copy-done.5
  3.8 0.1 multiply_add_fusion
  3.9 1.1 %fusion.2 = f32[8,64,2,64,1]{3,1,4,2,0:T(8,128)S(1)} fusion(f32[2,64,2,64,1]{3,1,0,2,4:T(8,128)S(1)} %copy-done, f32[1,8,64,64]{2,3,0,1:T(8,128)S(1)} %get-tuple-element.10, f32[1,8,64,64]{2,3,0,1:T(8,128)S(1)} %get-tuple-element.9), kind=kOutput, calls=%fused_computation.9 | convolution fusion | flops 100728832 | bytes 589824 | tf_op jit(solution)/shard_map/rcpn,rnsb->bcsp/dot_general | solution.py:238
  4.9 0.6 fusion.14
  5.6 0.1 fusion.51
  5.6 0.2 copy.50
  5.8 0.2 copy.51
  6.0 0.0 copy-start.2
  6.0 0.1 iota_compare_fusion.3
  6.1 0.1 copy.29
  6.3 0.7 %copy-done.2 = f32[128,256,1]{1,0,2:T(8,128)S(1)} copy-done((f32[128,256,1]{1,0,2:T(8,128)S(1)}, f32[128,256,1]{1,0,2:T(8,128)}, u32[]{:S(2)}) %copy-start.2) | copy-done | bytes 131096
  6.9 0.6 fusion.6
  7.6 0.3 fusion.33
  7.9 0.1 pad_maximum_fusion
  8.0 0.1 fusion.1
  8.1 0.9 %copy.35 = bf16[128,8,128]{2,1,0:T(8,128)(2,1)} copy(bf16[128,8,128]{2,0,1:T(8,128)(2,1)S(1)} %fusion.1) | data formatting | bytes 524288 | tf_op jit(solution)/shard_map/convert_element_type | solution.py:248
  9.0 0.6 copy.59
  9.6 0.1 copy-done.10
  9.7 0.6 copy.60
  10.3 47.9 %shard_map.163 = f32[64,2,128]{2,1,0:T(2,128)} custom-call(bf16[64,2,8,128]{3,2,1,0:T(8,128)(2,1)} %bitcast.70, bf16[2,144,512]{2,1,0:T(8,128)(2,1)} %constant.67.clone.table_ref, s32[2,2,512]{2,1,0:T(2,128)} %bitcast.79, f32[2,2,512]{2,1,0:T(2,128)} %bitcast.80, f32[2,512]{1,0:T(2,128)} %bitcast.78, s32[2,512]{1,0:T(2,128)} %bitcast.77), custom_call_target="tpu_custom_call" | custom-call | tf_op jit(solution)/shard_map/pallas_call | solution.py:251
  58.2 1.0 %reshape.131 = f32[128,2,64]{2,1,0:T(2,128)S(1)} reshape(f32[64,2,128]{2,1,0:T(2,128)} %shard_map.163) | data formatting | bytes 131072 | tf_op jit(solution)/shard_map/reshape | solution.py:274
  59.2 0.0 copy-start.13
  59.2 0.1 fusion.52
  59.3 0.6 copy-done.13
  60.0 0.5 fusion.23
  60.5 0.2 copy-done.12
  60.7 0.5 broadcast_select_fusion.1
  61.3 0.0 copy-start.1
  61.3 0.3 fusion.10
  61.6 0.6 copy-done.1
  62.2 0.3 convolution_bitcast_fusion.2
  62.4 0.5 copy-done.6
  62.9 0.0 copy-done.7
  62.9 0.4 convolution_bitcast_fusion.1
  63.3 0.0 copy-start.8
  63.3 0.1 reshape.133
  63.4 0.6 copy-done.8
  64.0 0.6 broadcast_multiply_fusion
  (14 shorter events, 0.1 us)
Async XLA Ops:
  0.0 0.7 %copy-start.11 = (s32[2,64]{1,0:T(2,128)S(1)}, s32[2,64]{1,0:T(2,128)}, u32[]{:S(2)}) copy-start(s32[2,64]{1,0:T(2,128)} %param.18) | copy-start | bytes 1540
  2.1 0.9 %copy-start = (f32[2,64,2,64,1]{3,1,0,2,4:T(8,128)S(1)}, f32[2,64,2,64,1]{3,1,0,2,4:T(8,128)}, u32[]{:S(2)}) copy-start(f32[2,64,2,64,1]{3,1,0,2,4:T(8,128)} %constant.82) | copy-start | bytes 196612
  2.1 0.9 %copy-start.3 = (f32[64,64]{0,1:T(8,128)S(1)}, f32[64,64]{0,1:T(8,128)}, u32[]{:S(2)}) copy-start(f32[64,64]{0,1:T(8,128)} %constant.75) | copy-start | bytes 49156
  3.0 0.8 %copy-start.4 = (f32[64,64]{0,1:T(8,128)S(1)}, f32[64,64]{0,1:T(8,128)}, u32[]{:S(2)}) copy-start(f32[64,64]{0,1:T(8,128)} %constant.64.clone) | copy-start | bytes 49156
  3.0 0.8 %copy-start.5 = (f32[64,64]{0,1:T(8,128)S(1)}, f32[64,64]{0,1:T(8,128)}, u32[]{:S(2)}) copy-start(f32[64,64]{0,1:T(8,128)} %constant.65.clone) | copy-start | bytes 49156
  6.0 0.9 %copy-start.2 = (f32[128,256,1]{1,0,2:T(8,128)S(1)}, f32[128,256,1]{1,0,2:T(8,128)}, u32[]{:S(2)}) copy-start(f32[128,256,1]{1,0,2:T(8,128)} %constant.83) | copy-start | bytes 393220
  8.1 0.9 %copy-start.9 = (s32[1,2,1,512]{3,2,1,0:T(1,128)S(1)}, s32[1,2,1,512]{3,2,1,0:T(1,128)}, u32[]{:S(2)}) copy-start(s32[1,2,1,512]{3,2,1,0:T(1,128)} %param.22) | copy-start | bytes 12292
  9.0 0.7 %copy-start.10 = (f32[1,2,1,512]{3,2,1,0:T(1,128)S(1)}, f32[1,2,1,512]{3,2,1,0:T(1,128)}, u32[]{:S(2)}) copy-start(f32[1,2,1,512]{3,2,1,0:T(1,128)} %param.21) | copy-start | bytes 12292
  59.2 0.8 %copy-start.13 = (f32[64,128]{1,0:T(8,128)S(1)}, f32[64,128]{1,0:T(8,128)}, u32[]{:S(2)}) copy-start(f32[64,128]{1,0:T(8,128)} %constant.76) | copy-start | bytes 98308
  60.0 0.8 %copy-start.12 = (f32[64,128]{1,0:T(8,128)S(1)}, f32[64,128]{1,0:T(8,128)}, u32[]{:S(2)}) copy-start(f32[64,128]{1,0:T(8,128)} %constant.77) | copy-start | bytes 98308
  61.3 0.9 %copy-start.1 = (f32[2,64,2,64]{3,1,0,2:T(8,128)S(1)}, f32[2,64,2,64]{3,1,0,2:T(8,128)}, u32[]{:S(2)}) copy-start(f32[2,64,2,64]{3,1,0,2:T(8,128)} %constant.69.clone) | copy-start | bytes 196612
  62.2 0.8 %copy-start.6 = (f32[1,64,64]{2,1,0:T(8,128)S(1)}, f32[1,64,64]{2,1,0:T(8,128)}, u32[]{:S(2)}) copy-start(f32[1,64,64]{2,1,0:T(8,128)} %constant.78) | copy-start | bytes 49156
  62.2 0.8 %copy-start.7 = (f32[1,64,64]{2,1,0:T(8,128)S(1)}, f32[1,64,64]{2,1,0:T(8,128)}, u32[]{:S(2)}) copy-start(f32[1,64,64]{2,1,0:T(8,128)} %constant.79) | copy-start | bytes 49156
  63.3 0.7 %copy-start.8 = (f32[4096]{0:T(1024)S(1)}, f32[4096]{0:T(1024)}, u32[]{:S(2)}) copy-start(f32[4096]{0:T(1024)} %constant.62.clone) | copy-start | bytes 49156

commit v2 on v1

v2 whole, which is shorter than its diff:
```python
import math

import jax
import jax.numpy as jnp
import numpy as np
from jax import lax
from jax.experimental import pallas as pl
from jax.experimental.pallas import tpu as pltpu
from jax.sharding import PartitionSpec as P

FN = 4096
CONTRIB = 64
FACET_ROWS = 8
COLS = 8
FRONTS = 2
SG = 512
VIS = 512
EXACT = lax.Precision.HIGHEST


def unit_table(length, rotation, rows, cols):
    angle = np.outer(np.arange(rows), np.arange(cols)) % length * (2.0 * np.pi / length)
    return np.cos(angle), rotation * np.sin(angle)


def real_form(cosine, sine):
    return np.block([[cosine, sine], [-sine, cosine]])


def f32(x):
    return jnp.asarray(np.asarray(x, np.float32))


def phase_table():
    cosine, sine = unit_table(SG, -1.0, CONTRIB, SG)
    cos8, sin8 = unit_table(8, -1.0, 8, SG)
    table = np.concatenate([cosine, sine, cos8, sin8], axis=0).astype(np.float32)
    high = table.astype(jnp.bfloat16)
    low = (table - high.astype(np.float32)).astype(jnp.bfloat16)
    return jnp.asarray(np.stack([high, low]))


def swapped(x):
    return jnp.concatenate([x[:, CONTRIB:], x[:, :CONTRIB]], axis=1)


def exact_dot(left, right, left_dim=1, right_dim=0):
    return lax.dot_general(
        left,
        right,
        (((left_dim,), (right_dim,)), ((), ())),
        precision=EXACT,
        preferred_element_type=jnp.float32,
    )


def major_kernel(
    strips_ref,
    offsets_ref,
    offsets_row_ref,
    tables_ref,
    turn_ref,
    window_ref,
    table_ref,
    cells_ref,
    values_ref,
    weights_ref,
    flags_ref,
    out_ref,
    staged_ref,
    leaving_ref,
    arrived_ref,
    phase_ref,
    back_ref,
    banded_ref,
    sum_ref,
    landed_ref,
    sems,
):
    facets = leaving_ref.shape[1]
    bands = back_ref.shape[1]
    groups = facets // FACET_ROWS
    windows = facets * FRONTS
    half = CONTRIB
    blocks = FN // CONTRIB
    me = lax.axis_index("facet")
    band = lax.axis_index("band")

    barrier = pltpu.get_barrier_semaphore()

    @pl.loop(1, facets)
    def _(k):
        pl.semaphore_signal(
            barrier, inc=1, device_id={"facet": lax.rem(me + 27 * k, facets)},
            device_id_type=pl.DeviceIdType.MESH,
        )

    @pl.loop(1, bands)
    def _(k):
        pl.semaphore_signal(
            barrier, inc=1, device_id={"band": lax.rem(band + k, bands)},
            device_id_type=pl.DeviceIdType.MESH,
        )

    offsets = offsets_ref[...]
    first = offsets >> 6
    shift = offsets & (half - 1)
    lane = lax.broadcasted_iota(jnp.int32, (windows, 2 * half), 1) & (half - 1)
    inside = lane >= shift
    angle = ((shift * lane) & (half - 1)).astype(jnp.float32) * (2.0 * math.pi / half)
    ramp_c = jnp.cos(angle)
    ramp_s = jnp.sin(angle)
    left_half = lax.broadcasted_iota(jnp.int32, (windows, 2 * half), 1) < half
    ramp_s = jnp.where(left_half, ramp_s, -ramp_s)
    block = lax.broadcasted_iota(jnp.int32, (windows, blocks), 1)
    pick = jnp.concatenate(
        [
            (block == first).astype(jnp.float32),
            (block == ((first + 1) & (blocks - 1))).astype(jnp.float32),
        ],
        axis=0,
    )
    section = exact_dot(tables_ref[0], strips_ref[...])
    tc = turn_ref[0]
    ts = turn_ref[1]
    turned_re = section[:half] * tc + section[half:] * ts
    turned_im = section[half:] * tc - section[:half] * ts
    for c in range(COLS):
        part = slice(half * c, half * (c + 1))
        pair = jnp.concatenate([turned_re[:, part], turned_im[:, part]], axis=1)
        spec = exact_dot(tables_ref[0], pair, 1, 1)
        spec = jnp.concatenate([spec[:half], spec[half:]], axis=1)
        chosen = exact_dot(pick, spec)
        cut = jnp.where(inside, chosen[:windows], chosen[windows:])
        piece = exact_dot(cut, tables_ref[1])
        piece = piece * ramp_c + swapped(piece) * ramp_s
        for t in range(FRONTS):
            staged_ref[t, :, c, :] = piece[facets * t : facets * (t + 1)]
    leaving_ref[...] = staged_ref[...].astype(jnp.bfloat16)

    pl.semaphore_wait(barrier, facets + bands - 2)

    def whole(ref, count, sem):
        part = ref.at[pl.ds(0, count)]
        pltpu.make_async_copy(part, part, sem).wait()

    owns = []
    for t in range(FRONTS):
        own = pltpu.make_async_copy(
            leaving_ref.at[t, me], arrived_ref.at[t, me], sems.at[8 + t]
        )
        own.start()
        owns.append(own)

        @pl.loop(1, facets)
        def _(k):
            to = lax.rem(me + 27 * k, facets)
            pltpu.make_async_remote_copy(
                src_ref=leaving_ref.at[t, to],
                dst_ref=arrived_ref.at[t, me],
                send_sem=sems.at[t],
                recv_sem=sems.at[2 + t],
                device_id={"facet": to},
                device_id_type=pl.DeviceIdType.MESH,
            ).start()

    for t in range(FRONTS):
        col = cells_ref[t, 1:2, :]
        hot = (lax.broadcasted_iota(jnp.int32, (SG, VIS), 0) == col).astype(jnp.float32)
        hot = hot.astype(jnp.bfloat16)
        phase_ref[t] = jnp.dot(
            table_ref[0], hot, preferred_element_type=jnp.float32
        ) + jnp.dot(table_ref[1], hot, preferred_element_type=jnp.float32)
    scale = SG ** (-0.5)
    returns = []
    for t in range(FRONTS):
        owns[t].wait()
        whole(leaving_ref.at[t], facets - 1, sems.at[t])
        whole(arrived_ref.at[t], facets - 1, sems.at[2 + t])
        row = cells_ref[t, 0:1, :]
        place = lax.broadcasted_iota(jnp.int32, (COLS * groups, VIS), 0)
        hot = (place == row).astype(jnp.float32).astype(jnp.bfloat16)
        turned = (row & 7) * groups + (row >> 3)
        hot_back = (place == turned).astype(jnp.float32).astype(jnp.bfloat16)
        er = phase_ref[t, 0:half, :]
        ei = phase_ref[t, half : 2 * half, :]
        pred_re = jnp.zeros((1, VIS), jnp.float32)
        pred_im = jnp.zeros((1, VIS), jnp.float32)
        for i in range(FACET_ROWS):
            slab = jnp.concatenate(
                [
                    arrived_ref[t, FACET_ROWS * j + i].astype(jnp.float32)
                    for j in range(groups)
                ],
                axis=0,
            ).astype(jnp.bfloat16)
            picked = lax.dot_general(
                slab, hot, (((0,), (0,)), ((), ())), preferred_element_type=jnp.float32
            )
            pr = picked[:half]
            pi = picked[half:]
            sr = jnp.sum(pr * er - pi * ei, axis=0, keepdims=True)
            si = jnp.sum(pr * ei + pi * er, axis=0, keepdims=True)
            c8 = phase_ref[t, 2 * half + i : 2 * half + i + 1, :]
            s8 = phase_ref[t, 2 * half + 8 + i : 2 * half + 9 + i, :]
            pred_re += c8 * sr - s8 * si
            pred_im += c8 * si + s8 * sr
        factor = weights_ref[t : t + 1, :] * flags_ref[t : t + 1, :].astype(jnp.float32)
        res_re = factor * (values_ref[t, 0:1, :] - scale * pred_re) * scale
        res_im = factor * (values_ref[t, 1:2, :] - scale * pred_im) * scale
        for i in range(FACET_ROWS):
            c8 = phase_ref[t, 2 * half + i : 2 * half + i + 1, :]
            s8 = phase_ref[t, 2 * half + 8 + i : 2 * half + 9 + i, :]
            gr = res_re * c8 + res_im * s8
            gi = res_im * c8 - res_re * s8
            wave = jnp.concatenate([gr * er + gi * ei, gi * er - gr * ei], axis=0)
            back = lax.dot_general(
                hot_back,
                wave.astype(jnp.bfloat16),
                (((1,), (1,)), ((), ())),
                preferred_element_type=jnp.float32,
            )
            back_ref[t, :, groups * i : groups * (i + 1), :] = back.reshape(
                COLS, groups, 2 * half
            ).astype(jnp.bfloat16)

        own = pltpu.make_async_copy(
            back_ref.at[t, band], banded_ref.at[t, band], sems.at[10 + t]
        )
        own.start()
        returns.append(own)

        @pl.loop(1, bands)
        def _(k):
            to = lax.rem(band + k, bands)
            pltpu.make_async_remote_copy(
                src_ref=back_ref.at[t, to],
                dst_ref=banded_ref.at[t, band],
                send_sem=sems.at[4 + t],
                recv_sem=sems.at[6 + t],
                device_id={"band": to},
                device_id_type=pl.DeviceIdType.MESH,
            ).start()

    for t in range(FRONTS):
        returns[t].wait()
        whole(back_ref.at[t], bands - 1, sems.at[4 + t])
        whole(banded_ref.at[t], bands - 1, sems.at[6 + t])
        total = banded_ref[t, 0].astype(jnp.float32)
        for b in range(1, bands):
            total += banded_ref[t, b].astype(jnp.float32)
        sum_ref[:, t, :] = total

    mine = lax.rem(me, FACET_ROWS) * groups + me // FACET_ROWS
    own = pltpu.make_async_copy(sum_ref.at[mine], landed_ref.at[me], sems.at[14])
    own.start()

    @pl.loop(1, facets)
    def _(k):
        to = lax.rem(me + 27 * k, facets)
        slot = lax.rem(to, FACET_ROWS) * groups + to // FACET_ROWS
        pltpu.make_async_remote_copy(
            src_ref=sum_ref.at[slot],
            dst_ref=landed_ref.at[me],
            send_sem=sems.at[12],
            recv_sem=sems.at[13],
            device_id={"facet": to},
            device_id_type=pl.DeviceIdType.MESH,
        ).start()

    own.wait()
    whole(sum_ref, facets - 1, sems.at[12])
    whole(landed_ref, facets - 1, sems.at[13])

    delivered = jnp.concatenate([landed_ref[:, t, :] for t in range(FRONTS)], axis=0)
    aligned = delivered * ramp_c - swapped(delivered) * ramp_s
    partial = exact_dot(aligned, tables_ref[2])
    first_row = offsets_row_ref[...] >> 6
    block_row = lax.broadcasted_iota(jnp.int32, (blocks, windows), 0)
    here = (block_row == first_row).astype(jnp.float32)
    after = (block_row == ((first_row + 1) & (blocks - 1))).astype(jnp.float32)
    spread = exact_dot(here, jnp.where(inside, partial, 0.0)) + exact_dot(
        after, jnp.where(inside, 0.0, partial)
    )
    both = exact_dot(tables_ref[3][:, :blocks], spread)
    crossed = swapped(both[half:])
    left_half = left_half[:half]
    line = both[:half] + jnp.where(left_half, -crossed, crossed)
    tc2 = tc[:, : 2 * half]
    ts2 = ts[:, : 2 * half]
    line = line * tc2 + swapped(line) * jnp.where(left_half, -ts2, ts2)
    out_ref[...] = exact_dot(tables_ref[4], line, 1, 1) * window_ref[...]


def local(facet_strips, subgrid_offsets, sample_cells, sample_values, sample_weights, sample_flags):
    vmem = pl.BlockSpec(memory_space=pltpu.VMEM)
    facets = lax.axis_size("facet")
    bands = lax.axis_size("band")
    windows = facets * FRONTS
    n = np.arange(FN)
    window = (1.0 + 0.5 * np.cos(2.0 * np.pi * n / FN)) * FN ** (-0.5)
    window = window.reshape(CONTRIB, CONTRIB)
    minus = real_form(*unit_table(CONTRIB, -1.0, CONTRIB, CONTRIB))
    plus = real_form(*unit_table(CONTRIB, 1.0, CONTRIB, CONTRIB))
    short = CONTRIB ** (-0.5)
    cosine, sine = unit_table(CONTRIB, 1.0, CONTRIB, CONTRIB)
    stacked = np.zeros((128, 128))
    stacked[:64, :64] = cosine
    stacked[64:, :64] = sine
    tables = np.stack([minus.T, plus * short, minus * short, stacked, plus.T])
    turn = np.stack([np.tile(x, (1, COLS)) for x in unit_table(FN, 1.0, CONTRIB, CONTRIB)])
    strips = facet_strips[0, 0].reshape(2, COLS, CONTRIB, CONTRIB) * f32(window)
    strips = jnp.transpose(strips, (0, 2, 1, 3)).reshape(2 * CONTRIB, COLS * CONTRIB)
    lines = pl.pallas_call(
        major_kernel,
        out_shape=jax.ShapeDtypeStruct((2 * CONTRIB, CONTRIB), jnp.float32),
        in_specs=[vmem] * 11,
        out_specs=vmem,
        scratch_shapes=[
            pltpu.VMEM((FRONTS, facets, COLS, 128), jnp.float32),
            pltpu.VMEM((FRONTS, facets, COLS, 128), jnp.bfloat16),
            pltpu.VMEM((FRONTS, facets, COLS, 128), jnp.bfloat16),
            pltpu.VMEM((FRONTS, 144, VIS), jnp.float32),
            pltpu.VMEM((FRONTS, bands, facets, 128), jnp.bfloat16),
            pltpu.VMEM((FRONTS, bands, facets, 128), jnp.bfloat16),
            pltpu.VMEM((facets, FRONTS, 128), jnp.float32),
            pltpu.VMEM((facets, FRONTS, 128), jnp.float32),
            pltpu.SemaphoreType.DMA((15,)),
        ],
        compiler_params=pltpu.CompilerParams(collective_id=0, has_side_effects=True),
    )(
        strips,
        subgrid_offsets.reshape(windows, 1),
        subgrid_offsets.reshape(1, windows),
        f32(tables),
        f32(turn),
        f32(np.concatenate([window, window], axis=0)),
        phase_table(),
        sample_cells.reshape(FRONTS, 2, VIS),
        sample_values.reshape(FRONTS, 2, VIS),
        sample_weights.reshape(FRONTS, VIS),
        sample_flags.reshape(FRONTS, VIS),
    )
    return lines.reshape(1, 1, 2, FN)


def solution(mesh):
    placed = (
        P("band", "facet", None, None, None),
        P(),
        P("band", None, "facet", None, None),
        P("band", None, "facet", None, None),
        P("band", None, "facet", None),
        P("band", None, "facet", None),
    )
    return jax.shard_map(
        local, mesh=mesh, in_specs=placed, out_specs=P("facet", "band", None, None), check_vma=False
    )
```

time: 65.3 us -> 55.8 us (0.85)
  matrix products: 4.92 us -> 0 us
  local copies, waits for them, and re-layouts: 10.2 us -> 6.29 us
  other arithmetic: 1.34 us -> 0.31 us
  Pallas kernels: 47.9 us -> 48.9 us
    unnamed x30 -> x10, local copies, waits for them, and re-layouts: 6.04 us -> 1.3 us
    dot_general x8 -> x0, matrix products: 4.59 us -> none  [the longest x2 1.05 us: local(): partial = jnp.dot(aligned, f32(minus), precision=EXACT)]
    reshape x3 -> x4, local copies, waits for them, and re-layouts: 1.22 us -> 3.84 us  [the longest x1 1.55 us: local(): return lines.reshape(1, 1, 2, FN)]
    squeeze x4 -> x0, local copies, waits for them, and re-layouts: 1.73 us -> none  [the longest x2 1.34 us: local(): facet_strips[0, 0] * f32(window)]
    another operation x0 -> x1, local copies, waits for them, and re-layouts: none -> 1.15 us  [local(): strips = facet_strips[0, 0].reshape(2, COLS, CONTRIB, CONTRIB) * f32(window)]
    pallas_call x1, Pallas kernels: 47.9 us -> 48.9 us  [local(): pl.pallas_call(major_kernel, out_shape=jax.ShapeDtypeStruct((2 * CONTRIB,...]
    convert_element_type x1 -> x0, local copies, waits for them, and re-layouts: 0.87 us -> none  [local(): leaving = piece.astype(jnp.bfloat16).reshape(facets, FRONTS, COLS, 128)]
where the time goes in v2:
time: 55.8 us; the launch traced here: 55.5 us
  Pallas kernels  48.9 us (88%)
  local copies, waits for them, and re-layouts  6.29 us (11%)
    pallas_call x1, Pallas kernels, local(): pl.pallas_call(major_kernel, out_shape=jax.ShapeDtypeStruct((2 * CONTRIB,...  48.9 us
    reshape x1, local copies, waits for them, and re-layouts, local(): return lines.reshape(1, 1, 2, FN)  1.55 us
    unnamed x10, local copies, waits for them, and re-layouts  1.3 us
    another operation x1, local copies, waits for them, and re-layouts, local(): strips = facet_strips[0, 0].reshape(2, COLS, CONTRIB, CONTRIB) * f32(window)  1.15 us

profile of v2, /device:TPU:1, one launch (start us, length us, event | category | flops | bytes accessed | tf_op | source)
XLA Modules:
  0.0 55.5 jit_solution(14387288161547312292)
XLA Ops:
  0.0 0.0 copy-start
  0.0 1.1 %reshape_squeeze.3 = f32[2,8,64,64]{3,2,1,0:T(8,128)S(1)} reshape(f32[1,1,2,8,4096]{4,3,2,1,0:T(8,128)} %param.11) | data formatting | bytes 524288 | tf_op jit(solution)/shard_map/reshape;squeeze | solution.py:312
  1.2 0.0 copy-done
  1.2 0.3 fusion
  1.5 0.0 copy-start.3
  1.5 0.9 %reshape.25.strips_ref = f32[128,512]{1,0:T(8,128)} reshape(f32[2,64,8,64]{3,2,1,0:T(8,128)S(1)} %fusion) | data formatting | bytes 524288 | tf_op jit(solution)/shard_map/reshape | solution.py:313
  2.4 0.0 copy-done.3
  2.4 0.0 copy-start.1
  2.4 0.8 %reshape.33.offsets_ref = s32[128,1]{1,0:T(8,128)} reshape(s32[2,64]{1,0:T(2,128)S(1)} %copy-done.3) | data formatting | bytes 1024 | tf_op jit(solution)/shard_map/reshape | solution.py:333
  3.1 0.0 copy-done.1
  3.1 0.0 copy-start.2
  3.1 0.6 %copy.23 = s32[1,2,1,512]{3,1,2,0:T(2,128)} copy(s32[1,2,1,512]{3,2,1,0:T(1,128)S(1)} %copy-done.1) | data formatting | bytes 8192
  3.7 0.1 copy-done.2
  3.8 0.6 %copy.24 = f32[1,2,1,512]{3,1,2,0:T(2,128)} copy(f32[1,2,1,512]{3,2,1,0:T(1,128)S(1)} %copy-done.2) | data formatting | bytes 8192
  4.4 0.7 %reshape.27.offsets_row_ref = s32[1,128]{1,0:T(1,128)} reshape(s32[2,64]{1,0:T(2,128)S(1)} %copy-done.3) | data formatting | bytes 1024 | tf_op jit(solution)/shard_map/reshape | solution.py:334
  5.1 48.9 %shard_map.109 = f32[128,64]{1,0:T(8,128)} custom-call(f32[128,512]{1,0:T(8,128)} %reshape.25.strips_ref, s32[128,1]{1,0:T(8,128)} %reshape.33.offsets_ref, s32[1,128]{1,0:T(1,128)} %reshape.27.offsets_row_ref, f32[5,128,128]{2,1,0:T(8,128)} %constant.11.clone.tables_ref, f32[2,64,512]{2,1,0:T(8,128)} %constant.12.clone.turn_ref, ...), custom_call_target="tpu_custom_call" | custom-call | tf_op jit(solution)/shard_map/pallas_call | solution.py:314
  54.0 1.5 %reshape.32 = f32[1,1,2,4096]{3,2,1,0:T(2,128)} reshape(f32[128,64]{1,0:T(8,128)} %shard_map.109) | data formatting | bytes 65536 | tf_op jit(solution)/shard_map/reshape | solution.py:344
Async XLA Ops:
  0.0 1.2 %copy-start = (f32[64,64]{1,0:T(8,128)S(1)}, f32[64,64]{1,0:T(8,128)}, u32[]{:S(2)}) copy-start(f32[64,64]{1,0:T(8,128)} %constant.10.clone) | copy-start | bytes 49156
  1.5 0.9 %copy-start.3 = (s32[2,64]{1,0:T(2,128)S(1)}, s32[2,64]{1,0:T(2,128)}, u32[]{:S(2)}) copy-start(s32[2,64]{1,0:T(2,128)} %param.12) | copy-start | bytes 1540
  2.4 0.8 %copy-start.1 = (s32[1,2,1,512]{3,2,1,0:T(1,128)S(1)}, s32[1,2,1,512]{3,2,1,0:T(1,128)}, u32[]{:S(2)}) copy-start(s32[1,2,1,512]{3,2,1,0:T(1,128)} %param.16) | copy-start | bytes 12292
  3.1 0.7 %copy-start.2 = (f32[1,2,1,512]{3,2,1,0:T(1,128)S(1)}, f32[1,2,1,512]{3,2,1,0:T(1,128)}, u32[]{:S(2)}) copy-start(f32[1,2,1,512]{3,2,1,0:T(1,128)} %param.15) | copy-start | bytes 12292

commit v3 on v2

v3 whole, which is shorter than its diff:
```python
import math

import jax
import jax.numpy as jnp
import numpy as np
from jax import lax
from jax.experimental import pallas as pl
from jax.experimental.pallas import tpu as pltpu
from jax.sharding import PartitionSpec as P

FN = 4096
CONTRIB = 64
FACET_ROWS = 8
COLS = 8
FRONTS = 2
SG = 512
VIS = 512
ROW = 4
DEEP = 8
EXACT = lax.Precision.HIGHEST


def unit_table(length, rotation, rows, cols):
    angle = np.outer(np.arange(rows), np.arange(cols)) % length * (2.0 * np.pi / length)
    return np.cos(angle), rotation * np.sin(angle)


def real_form(cosine, sine):
    return np.block([[cosine, sine], [-sine, cosine]])


def f32(x):
    return jnp.asarray(np.asarray(x, np.float32))


def phase_table():
    cosine, sine = unit_table(SG, -1.0, CONTRIB, SG)
    cos8, sin8 = unit_table(8, -1.0, 8, SG)
    table = np.concatenate([cosine, sine, cos8, sin8], axis=0).astype(np.float32)
    high = table.astype(jnp.bfloat16)
    low = (table - high.astype(np.float32)).astype(jnp.bfloat16)
    return jnp.asarray(np.stack([high, low]))


def swapped(x):
    return jnp.concatenate([x[:, CONTRIB:], x[:, :CONTRIB]], axis=1)


def exact_dot(left, right, left_dim=1, right_dim=0):
    return lax.dot_general(
        left,
        right,
        (((left_dim,), (right_dim,)), ((), ())),
        precision=EXACT,
        preferred_element_type=jnp.float32,
    )


def split_index(facet, deep):
    across = facet // (ROW * deep) * ROW + facet % ROW
    return across, facet // ROW % deep


def major_kernel(
    strips_ref,
    offsets_ref,
    tables_ref,
    split_ref,
    turn_ref,
    window_ref,
    table_ref,
    cells_ref,
    values_ref,
    weights_ref,
    flags_ref,
    out_ref,
    strip_ref,
    staged_ref,
    leaving_ref,
    middle_ref,
    arrived_ref,
    phase_ref,
    back_ref,
    banded_ref,
    sum_ref,
    passing_ref,
    landed_ref,
    placed_ref,
    sems,
):
    deep = leaving_ref.shape[1]
    wide = leaving_ref.shape[2]
    facets = deep * wide
    bands = back_ref.shape[1]
    groups = facets // FACET_ROWS
    windows = facets * FRONTS
    half = CONTRIB
    blocks = FN // CONTRIB
    me = lax.axis_index("facet")
    band = lax.axis_index("band")
    z = lax.rem(me // ROW, deep)
    w = me // (ROW * deep) * ROW + lax.rem(me, ROW)

    def along_z(to):
        return {"facet": (w // ROW * deep + to) * ROW + lax.rem(w, ROW)}

    def along_w(to):
        return {"facet": (to // ROW * deep + z) * ROW + lax.rem(to, ROW)}

    def along_band(to):
        return {"band": to}

    ways = ((z, deep, along_z), (w, wide, along_w), (band, bands, along_band))

    barrier = pltpu.get_barrier_semaphore()

    for mine, count, device in ways:

        @pl.loop(1, count)
        def _(k):
            pl.semaphore_signal(
                barrier, inc=1, device_id=device(lax.rem(mine + k, count)),
                device_id_type=pl.DeviceIdType.MESH,
            )

    line_index = lax.broadcasted_iota(jnp.int32, (facets, facets), 0)
    diagonal = line_index == lax.broadcasted_iota(jnp.int32, (facets, facets), 1)
    offsets = jnp.concatenate(
        [
            jnp.sum(jnp.where(diagonal, offsets_ref[t : t + 1, :], 0), axis=1, keepdims=True)
            for t in range(FRONTS)
        ],
        axis=0,
    )
    first = offsets >> 6
    shift = offsets & (half - 1)
    lane = lax.broadcasted_iota(jnp.int32, (windows, 2 * half), 1) & (half - 1)
    inside = lane >= shift
    angle = ((shift * lane) & (half - 1)).astype(jnp.float32) * (2.0 * math.pi / half)
    ramp_c = jnp.cos(angle)
    ramp_s = jnp.sin(angle)
    left_half = lax.broadcasted_iota(jnp.int32, (windows, 2 * half), 1) < half
    ramp_s = jnp.where(left_half, ramp_s, -ramp_s)
    block = lax.broadcasted_iota(jnp.int32, (windows, blocks), 1)
    pick = jnp.concatenate(
        [
            (block == first).astype(jnp.float32),
            (block == ((first + 1) & (blocks - 1))).astype(jnp.float32),
        ],
        axis=0,
    )
    chunks = FN // 128
    for r in range(2):
        for a in range(chunks):
            strip_ref[chunks * r + a] = strips_ref[r, :, 128 * a : 128 * (a + 1)]
    tc2 = turn_ref[0]
    ts2 = turn_ref[1]
    tc = tc2[:, :half]
    ts = ts2[:, :half]
    for c in range(COLS):
        section = exact_dot(split_ref[...], strip_ref[:, c, :] * window_ref[...])
        section = section[:128] + swapped(section[128:])
        section = section[:, :half]
        pair = jnp.concatenate(
            [
                section[:half] * tc + section[half:] * ts,
                section[half:] * tc - section[:half] * ts,
            ],
            axis=1,
        )
        spec = exact_dot(tables_ref[0], pair, 1, 1)
        spec = jnp.concatenate([spec[:half], spec[half:]], axis=1)
        chosen = exact_dot(pick, spec)
        cut = jnp.where(inside, chosen[:windows], chosen[windows:])
        piece = exact_dot(cut, tables_ref[1])
        piece = piece * ramp_c + swapped(piece) * ramp_s
        for t in range(FRONTS):
            staged_ref[t, :, c, :] = piece[facets * t : facets * (t + 1)]
    for t in range(FRONTS):
        for a in range(facets // ROW):
            leaving_ref[t, a % deep, a // deep * ROW : (a // deep + 1) * ROW] = staged_ref[
                t, ROW * a : ROW * (a + 1)
            ].astype(jnp.bfloat16)

    pl.semaphore_wait(barrier, deep + wide + bands - 3)

    def whole(ref, count, sem):
        part = ref.at[pl.ds(0, count)]
        pltpu.make_async_copy(part, part, sem).wait()

    def begin(way, source, target, base):
        mine, count, device = way
        own = pltpu.make_async_copy(source(mine), target, sems.at[base + 2])
        own.start()

        @pl.loop(1, count)
        def _(k):
            to = lax.rem(mine + k, count)
            pltpu.make_async_remote_copy(
                src_ref=source(to),
                dst_ref=target,
                send_sem=sems.at[base],
                recv_sem=sems.at[base + 1],
                device_id=device(to),
                device_id_type=pl.DeviceIdType.MESH,
            ).start()

        return own

    def finish(own, way, sent, landed, base):
        own.wait()
        whole(sent, way[1] - 1, sems.at[base])
        whole(landed, way[1] - 1, sems.at[base + 1])

    owns = [
        begin(ways[0], lambda to: leaving_ref.at[t, to], middle_ref.at[t, z], 3 * t)
        for t in range(FRONTS)
    ]
    for t in range(FRONTS):
        col = cells_ref[t, 1:2, :]
        hot = (lax.broadcasted_iota(jnp.int32, (SG, VIS), 0) == col).astype(jnp.float32)
        hot = hot.astype(jnp.bfloat16)
        phase_ref[t] = jnp.dot(
            table_ref[0], hot, preferred_element_type=jnp.float32
        ) + jnp.dot(table_ref[1], hot, preferred_element_type=jnp.float32)
    seconds = []
    for t in range(FRONTS):
        finish(owns[t], ways[0], leaving_ref.at[t], middle_ref.at[t], 3 * t)
        seconds.append(
            begin(ways[1], lambda to: middle_ref.at[t, :, to], arrived_ref.at[t, w], 6 + 3 * t)
        )
    scale = SG ** (-0.5)
    returns = []
    for t in range(FRONTS):
        finish(seconds[t], ways[1], middle_ref.at[t], arrived_ref.at[t], 6 + 3 * t)
        row = cells_ref[t, 0:1, :]
        place = lax.broadcasted_iota(jnp.int32, (COLS * groups, VIS), 0)
        hot = (place == row).astype(jnp.float32).astype(jnp.bfloat16)
        turned = (row & 7) * groups + (row >> 3)
        hot_back = (place == turned).astype(jnp.float32).astype(jnp.bfloat16)
        er = phase_ref[t, 0:half, :]
        ei = phase_ref[t, half : 2 * half, :]
        pred_re = jnp.zeros((1, VIS), jnp.float32)
        pred_im = jnp.zeros((1, VIS), jnp.float32)
        for i in range(FACET_ROWS):
            slab = jnp.concatenate(
                [
                    arrived_ref[(t,) + split_index(FACET_ROWS * j + i, deep)].astype(jnp.float32)
                    for j in range(groups)
                ],
                axis=0,
            ).astype(jnp.bfloat16)
            picked = lax.dot_general(
                slab, hot, (((0,), (0,)), ((), ())), preferred_element_type=jnp.float32
            )
            pr = picked[:half]
            pi = picked[half:]
            sr = jnp.sum(pr * er - pi * ei, axis=0, keepdims=True)
            si = jnp.sum(pr * ei + pi * er, axis=0, keepdims=True)
            c8 = phase_ref[t, 2 * half + i : 2 * half + i + 1, :]
            s8 = phase_ref[t, 2 * half + 8 + i : 2 * half + 9 + i, :]
            pred_re += c8 * sr - s8 * si
            pred_im += c8 * si + s8 * sr
        factor = weights_ref[t] * flags_ref[t].astype(jnp.float32)
        res_re = factor * (values_ref[t, 0:1, :] - scale * pred_re) * scale
        res_im = factor * (values_ref[t, 1:2, :] - scale * pred_im) * scale
        for i in range(FACET_ROWS):
            c8 = phase_ref[t, 2 * half + i : 2 * half + i + 1, :]
            s8 = phase_ref[t, 2 * half + 8 + i : 2 * half + 9 + i, :]
            gr = res_re * c8 + res_im * s8
            gi = res_im * c8 - res_re * s8
            wave = jnp.concatenate([gr * er + gi * ei, gi * er - gr * ei], axis=0)
            back = lax.dot_general(
                hot_back,
                wave.astype(jnp.bfloat16),
                (((1,), (1,)), ((), ())),
                preferred_element_type=jnp.float32,
            )
            back_ref[t, :, groups * i : groups * (i + 1), :] = back.reshape(
                COLS, groups, 2 * half
            ).astype(jnp.bfloat16)

        returns.append(
            begin(
                ways[2], lambda to: back_ref.at[t, to], banded_ref.at[t, band], 12 + 3 * t
            )
        )

    for t in range(FRONTS):
        finish(returns[t], ways[2], back_ref.at[t], banded_ref.at[t], 12 + 3 * t)
        total = banded_ref[t, 0].astype(jnp.float32)
        for b in range(1, bands):
            total += banded_ref[t, b].astype(jnp.float32)
        for f in range(facets):
            slot = f % FACET_ROWS * groups + f // FACET_ROWS
            across, along = split_index(f, deep)
            sum_ref[along, across, t : t + 1, :] = total[slot : slot + 1]

    own = begin(ways[0], lambda to: sum_ref.at[to], passing_ref.at[z], 18)
    finish(own, ways[0], sum_ref, passing_ref, 18)
    own = begin(ways[1], lambda to: passing_ref.at[:, to], landed_ref.at[w], 21)
    finish(own, ways[1], passing_ref, landed_ref, 21)

    for t in range(FRONTS):
        for f in range(facets):
            across, along = split_index(f, deep)
            placed_ref[facets * t + f : facets * t + f + 1, :] = landed_ref[
                across, along, t : t + 1, :
            ]
    delivered = placed_ref[...]
    aligned = delivered * ramp_c - swapped(delivered) * ramp_s
    partial = exact_dot(aligned, tables_ref[2])
    first_row = (
        jnp.concatenate([offsets_ref[t : t + 1, :] for t in range(FRONTS)], axis=1) >> 6
    )
    block_row = lax.broadcasted_iota(jnp.int32, (blocks, windows), 0)
    here = (block_row == first_row).astype(jnp.float32)
    after = (block_row == ((first_row + 1) & (blocks - 1))).astype(jnp.float32)
    spread = exact_dot(here, jnp.where(inside, partial, 0.0)) + exact_dot(
        after, jnp.where(inside, 0.0, partial)
    )
    both = exact_dot(tables_ref[3][:, :blocks], spread)
    crossed = swapped(both[half:])
    left_half = left_half[:half]
    line = both[:half] + jnp.where(left_half, -crossed, crossed)
    line = line * tc2 + swapped(line) * jnp.where(left_half, -ts2, ts2)
    ends = exact_dot(tables_ref[4], line, 1, 1)
    ends = jnp.concatenate([ends[:half], ends[half:]], axis=1) * window_ref[...]
    for r in range(2):
        for a in range(chunks):
            out_ref[r : r + 1, 128 * a : 128 * (a + 1)] = ends[
                chunks * r + a : chunks * r + a + 1
            ]


def local(facet_strips, subgrid_offsets, sample_cells, sample_values, sample_weights, sample_flags):
    vmem = pl.BlockSpec(memory_space=pltpu.VMEM)
    facets = lax.axis_size("facet")
    bands = lax.axis_size("band")
    wide = facets // DEEP
    n = np.arange(FN)
    window = (1.0 + 0.5 * np.cos(2.0 * np.pi * n / FN)) * FN ** (-0.5)
    window = np.tile(window.reshape(FN // 128, 128), (2, 1))
    minus = real_form(*unit_table(CONTRIB, -1.0, CONTRIB, CONTRIB))
    plus = real_form(*unit_table(CONTRIB, 1.0, CONTRIB, CONTRIB))
    short = CONTRIB ** (-0.5)
    cosine, sine = unit_table(CONTRIB, 1.0, CONTRIB, CONTRIB)
    stacked = np.zeros((128, 128))
    stacked[:64, :64] = cosine
    stacked[64:, :64] = sine
    ends = plus.T.reshape(2, CONTRIB, 128)
    ordered = np.concatenate([ends[:, 0::2].reshape(64, 128), ends[:, 1::2].reshape(64, 128)])
    tables = np.stack([minus.T, plus * short, minus * short, stacked, ordered])
    split = np.concatenate([minus.T[:, 0::2], minus.T[:, 1::2]], axis=0)
    turn = np.stack([np.tile(x, (1, 2)) for x in unit_table(FN, 1.0, CONTRIB, CONTRIB)])
    lines = pl.pallas_call(
        major_kernel,
        out_shape=jax.ShapeDtypeStruct((2, FN), jnp.float32),
        in_specs=[vmem] * 11,
        out_specs=vmem,
        scratch_shapes=[
            pltpu.VMEM((2 * FN // 128, COLS, 128), jnp.float32),
            pltpu.VMEM((FRONTS, facets, COLS, 128), jnp.float32),
            pltpu.VMEM((FRONTS, DEEP, wide, COLS, 128), jnp.bfloat16),
            pltpu.VMEM((FRONTS, DEEP, wide, COLS, 128), jnp.bfloat16),
            pltpu.VMEM((FRONTS, wide, DEEP, COLS, 128), jnp.bfloat16),
            pltpu.VMEM((FRONTS, 144, VIS), jnp.float32),
            pltpu.VMEM((FRONTS, bands, facets, 128), jnp.bfloat16),
            pltpu.VMEM((FRONTS, bands, facets, 128), jnp.bfloat16),
            pltpu.VMEM((DEEP, wide, FRONTS, 128), jnp.float32),
            pltpu.VMEM((DEEP, wide, FRONTS, 128), jnp.float32),
            pltpu.VMEM((wide, DEEP, FRONTS, 128), jnp.float32),
            pltpu.VMEM((FRONTS * facets, 128), jnp.float32),
            pltpu.SemaphoreType.DMA((24,)),
        ],
        compiler_params=pltpu.CompilerParams(collective_id=0, has_side_effects=True),
    )(
        facet_strips.reshape(2, COLS, FN),
        subgrid_offsets,
        f32(tables),
        f32(split),
        f32(turn),
        f32(window),
        phase_table(),
        sample_cells.reshape(FRONTS, 2, VIS),
        sample_values.reshape(FRONTS, 2, VIS),
        sample_weights.reshape(FRONTS, 1, VIS),
        sample_flags.reshape(FRONTS, 1, VIS),
    )
    return lines.reshape(1, 1, 2, FN)


def solution(mesh):
    placed = (
        P("band", "facet", None, None, None),
        P(),
        P("band", None, "facet", None, None),
        P("band", None, "facet", None, None),
        P("band", None, "facet", None),
        P("band", None, "facet", None),
    )
    return jax.shard_map(
        local, mesh=mesh, in_specs=placed, out_specs=P("facet", "band", None, None), check_vma=False
    )
```

time: 55.8 us -> 56.9 us (1.020)
  the two profiles are of different devices: /device:TPU:1 before, /device:TPU:56 now
where the time goes in v3:
time: 56.9 us; the launch traced here: 56.7 us
  Pallas kernels  55.3 us (97%)
  local copies, waits for them, and re-layouts  1.38 us (2%)
    pallas_call x1, Pallas kernels, local(): pl.pallas_call(major_kernel, out_shape=jax.ShapeDtypeStruct((2, FN), jnp....  55.3 us
    unnamed x1, local copies, waits for them, and re-layouts  1.38 us

profile of v3, /device:TPU:56, one launch (start us, length us, event | category | flops | bytes accessed | tf_op | source)
XLA Modules:
  0.0 56.7 jit_solution(1905519808962789991)
XLA Ops:
  0.0 55.3 %shard_map.109 = f32[2,4096]{1,0:T(2,128)} custom-call(f32[2,8,4096]{2,1,0:T(8,128)} %bitcast.6, s32[2,64]{1,0:T(2,128)} %offsets_ref.1, f32[5,128,128]{2,1,0:T(8,128)} %constant.10.clone.tables_ref, f32[256,64]{1,0:T(8,128)} %constant.11.clone.split_ref, f32[2,64,128]{2,1,0:T(8,128)} %constant.12.clone.turn_ref, f32[64,128]{1,0:T(8,128)} %constant.13.clone.window_ref, ...), custom_call_target="tpu_custom_call" | custom-call | tf_op jit(solution)/shard_map/pallas_call | solution.py:356
  55.3 1.4 %copy.13 = f32[1,1,2,4096]{3,2,1,0:T(2,128)} copy(f32[1,1,2,4096]{3,2,1,0:T(2,128)} %bitcast.7) | data formatting | bytes 65536

commit v4 on v2

--- a/solution.py
+++ b/solution.py
@@ -15,6 +15,8 @@
 FRONTS = 2
 SG = 512
 VIS = 512
+ROW = 4
+DEEP = 8
 EXACT = lax.Precision.HIGHEST
 
 
@@ -57,8 +59,8 @@
 def major_kernel(
     strips_ref,
     offsets_ref,
-    offsets_row_ref,
     tables_ref,
+    split_ref,
     turn_ref,
     window_ref,
     table_ref,
@@ -67,6 +69,7 @@
     weights_ref,
     flags_ref,
     out_ref,
+    strip_ref,
     staged_ref,
     leaving_ref,
     arrived_ref,
@@ -76,6 +79,7 @@
     sum_ref,
     landed_ref,
     sems,
+    ready,
 ):
     facets = leaving_ref.shape[1]
     bands = back_ref.shape[1]
@@ -85,24 +89,43 @@
     blocks = FN // CONTRIB
     me = lax.axis_index("facet")
     band = lax.axis_index("band")
+    wide = facets // DEEP
+    z = lax.rem(me // ROW, DEEP)
+    w = me // (ROW * DEEP) * ROW + lax.rem(me, ROW)
+
+    def along_z(to):
+        return {"facet": (w // ROW * DEEP + to) * ROW + lax.rem(w, ROW)}
+
+    def along_w(to):
+        return {"facet": (to // ROW * DEEP + z) * ROW + lax.rem(to, ROW)}
+
+    def along_band(to):
+        return {"band": to}
+
+    def greet(semaphore, mine, count, device):
+        @pl.loop(1, count)
+        def _(k):
+            pl.semaphore_signal(
+                semaphore, inc=1, device_id=device(lax.rem(mine + k, count)),
+                device_id_type=pl.DeviceIdType.MESH,
+            )
+
 
     barrier = pltpu.get_barrier_semaphore()
 
-    @pl.loop(1, facets)
-    def _(k):
-        pl.semaphore_signal(
-            barrier, inc=1, device_id={"facet": lax.rem(me + 27 * k, facets)},
-            device_id_type=pl.DeviceIdType.MESH,
-        )
-
-    @pl.loop(1, bands)
-    def _(k):
-        pl.semaphore_signal(
-            barrier, inc=1, device_id={"band": lax.rem(band + k, bands)},
-            device_id_type=pl.DeviceIdType.MESH,
-        )
-
-    offsets = offsets_ref[...]
+    greet(barrier, w, wide, along_w)
+    greet(barrier, z, DEEP, along_z)
+    greet(barrier, band, bands, along_band)
+
+    line_index = lax.broadcasted_iota(jnp.int32, (facets, facets), 0)
+    diagonal = line_index == lax.broadcasted_iota(jnp.int32, (facets, facets), 1)
+    offsets = jnp.concatenate(
+        [
+            jnp.sum(jnp.where(diagonal, offsets_ref[t : t + 1, :], 0), axis=1, keepdims=True)
+            for t in range(FRONTS)
+        ],
+        axis=0,
+    )
     first = offsets >> 6
     shift = offsets & (half - 1)
     lane = lax.broadcasted_iota(jnp.int32, (windows, 2 * half), 1) & (half - 1)
@@ -120,14 +143,28 @@
         ],
         axis=0,
     )
-    section = exact_dot(tables_ref[0], strips_ref[...])
-    tc = turn_ref[0]
-    ts = turn_ref[1]
-    turned_re = section[:half] * tc + section[half:] * ts
-    turned_im = section[half:] * tc - section[:half] * ts
+    chunks = FN // 128
+    for r in range(2):
+        for a in range(chunks):
+            strip_ref[chunks * r + a] = strips_ref[r, :, 128 * a : 128 * (a + 1)]
+    tc2 = turn_ref[0]
+    ts2 = turn_ref[1]
+    tc = tc2[:, :half]
+    ts = ts2[:, :half]
     for c in range(COLS):
-        part = slice(half * c, half * (c + 1))
-        pair = jnp.concatenate([turned_re[:, part], turned_im[:, part]], axis=1)
+        if c == COLS // 2:
+            pl.semaphore_wait(barrier, wide + DEEP + bands - 3)
+            greet(ready, z, DEEP, along_z)
+        section = exact_dot(split_ref[...], strip_ref[:, c, :] * window_ref[...])
+        section = section[:128] + swapped(section[128:])
+        section = section[:, :half]
+        pair = jnp.concatenate(
+            [
+                section[:half] * tc + section[half:] * ts,
+                section[half:] * tc - section[:half] * ts,
+            ],
+            axis=1,
+        )
         spec = exact_dot(tables_ref[0], pair, 1, 1)
         spec = jnp.concatenate([spec[:half], spec[half:]], axis=1)
         chosen = exact_dot(pick, spec)
@@ -138,7 +175,7 @@
             staged_ref[t, :, c, :] = piece[facets * t : facets * (t + 1)]
     leaving_ref[...] = staged_ref[...].astype(jnp.bfloat16)
 
-    pl.semaphore_wait(barrier, facets + bands - 2)
+    pl.semaphore_wait(ready, DEEP - 1)
 
     def whole(ref, count, sem):
         part = ref.at[pl.ds(0, count)]
@@ -205,7 +242,7 @@
             s8 = phase_ref[t, 2 * half + 8 + i : 2 * half + 9 + i, :]
             pred_re += c8 * sr - s8 * si
             pred_im += c8 * si + s8 * sr
-        factor = weights_ref[t : t + 1, :] * flags_ref[t : t + 1, :].astype(jnp.float32)
+        factor = weights_ref[t] * flags_ref[t].astype(jnp.float32)
         res_re = factor * (values_ref[t, 0:1, :] - scale * pred_re) * scale
         res_im = factor * (values_ref[t, 1:2, :] - scale * pred_im) * scale
         for i in range(FACET_ROWS):
@@ -275,7 +312,9 @@
     delivered = jnp.concatenate([landed_ref[:, t, :] for t in range(FRONTS)], axis=0)
     aligned = delivered * ramp_c - swapped(delivered) * ramp_s
     partial = exact_dot(aligned, tables_ref[2])
-    first_row = offsets_row_ref[...] >> 6
+    first_row = (
+        jnp.concatenate([offsets_ref[t : t + 1, :] for t in range(FRONTS)], axis=1) >> 6
+    )
     block_row = lax.broadcasted_iota(jnp.int32, (blocks, windows), 0)
     here = (block_row == first_row).astype(jnp.float32)
     after = (block_row == ((first_row + 1) & (blocks - 1))).astype(jnp.float32)
@@ -286,20 +325,23 @@
     crossed = swapped(both[half:])
     left_half = left_half[:half]
     line = both[:half] + jnp.where(left_half, -crossed, crossed)
-    tc2 = tc[:, : 2 * half]
-    ts2 = ts[:, : 2 * half]
     line = line * tc2 + swapped(line) * jnp.where(left_half, -ts2, ts2)
-    out_ref[...] = exact_dot(tables_ref[4], line, 1, 1) * window_ref[...]
+    ends = exact_dot(tables_ref[4], line, 1, 1)
+    ends = jnp.concatenate([ends[:half], ends[half:]], axis=1) * window_ref[...]
+    for r in range(2):
+        for a in range(chunks):
+            out_ref[r : r + 1, 128 * a : 128 * (a + 1)] = ends[
+                chunks * r + a : chunks * r + a + 1
+            ]
 
 
 def local(facet_strips, subgrid_offsets, sample_cells, sample_values, sample_weights, sample_flags):
     vmem = pl.BlockSpec(memory_space=pltpu.VMEM)
     facets = lax.axis_size("facet")
     bands = lax.axis_size("band")
-    windows = facets * FRONTS
     n = np.arange(FN)
     window = (1.0 + 0.5 * np.cos(2.0 * np.pi * n / FN)) * FN ** (-0.5)
-    window = window.reshape(CONTRIB, CONTRIB)
+    window = np.tile(window.reshape(FN // 128, 128), (2, 1))
     minus = real_form(*unit_table(CONTRIB, -1.0, CONTRIB, CONTRIB))
     plus = real_form(*unit_table(CONTRIB, 1.0, CONTRIB, CONTRIB))
     short = CONTRIB ** (-0.5)
@@ -307,16 +349,18 @@
     stacked = np.zeros((128, 128))
     stacked[:64, :64] = cosine
     stacked[64:, :64] = sine
-    tables = np.stack([minus.T, plus * short, minus * short, stacked, plus.T])
-    turn = np.stack([np.tile(x, (1, COLS)) for x in unit_table(FN, 1.0, CONTRIB, CONTRIB)])
-    strips = facet_strips[0, 0].reshape(2, COLS, CONTRIB, CONTRIB) * f32(window)
-    strips = jnp.transpose(strips, (0, 2, 1, 3)).reshape(2 * CONTRIB, COLS * CONTRIB)
+    ends = plus.T.reshape(2, CONTRIB, 128)
+    ordered = np.concatenate([ends[:, 0::2].reshape(64, 128), ends[:, 1::2].reshape(64, 128)])
+    tables = np.stack([minus.T, plus * short, minus * short, stacked, ordered])
+    split = np.concatenate([minus.T[:, 0::2], minus.T[:, 1::2]], axis=0)
+    turn = np.stack([np.tile(x, (1, 2)) for x in unit_table(FN, 1.0, CONTRIB, CONTRIB)])
     lines = pl.pallas_call(
         major_kernel,
-        out_shape=jax.ShapeDtypeStruct((2 * CONTRIB, CONTRIB), jnp.float32),
+        out_shape=jax.ShapeDtypeStruct((2, FN), jnp.float32),
         in_specs=[vmem] * 11,
         out_specs=vmem,
         scratch_shapes=[
+            pltpu.VMEM((2 * FN // 128, COLS, 128), jnp.float32),
             pltpu.VMEM((FRONTS, facets, COLS, 128), jnp.float32),
             pltpu.VMEM((FRONTS, facets, COLS, 128), jnp.bfloat16),
             pltpu.VMEM((FRONTS, facets, COLS, 128), jnp.bfloat16),
@@ -326,20 +370,21 @@
             pltpu.VMEM((facets, FRONTS, 128), jnp.float32),
             pltpu.VMEM((facets, FRONTS, 128), jnp.float32),
             pltpu.SemaphoreType.DMA((15,)),
+            pltpu.SemaphoreType.REGULAR,
         ],
         compiler_params=pltpu.CompilerParams(collective_id=0, has_side_effects=True),
     )(
-        strips,
-        subgrid_offsets.reshape(windows, 1),
-        subgrid_offsets.reshape(1, windows),
+        facet_strips.reshape(2, COLS, FN),
+        subgrid_offsets,
         f32(tables),
+        f32(split),
         f32(turn),
-        f32(np.concatenate([window, window], axis=0)),
+        f32(window),
         phase_table(),
         sample_cells.reshape(FRONTS, 2, VIS),
         sample_values.reshape(FRONTS, 2, VIS),
-        sample_weights.reshape(FRONTS, VIS),
-        sample_flags.reshape(FRONTS, VIS),
+        sample_weights.reshape(FRONTS, 1, VIS),
+        sample_flags.reshape(FRONTS, 1, VIS),
     )
     return lines.reshape(1, 1, 2, FN)
 

time: 55.8 us -> 51.7 us (0.927)
  local copies, waits for them, and re-layouts: 6.29 us -> 1.38 us
  Pallas kernels: 48.9 us -> 49.8 us
    reshape x4 -> x0, local copies, waits for them, and re-layouts: 3.84 us -> none  [the longest x1 1.55 us: local(): return lines.reshape(1, 1, 2, FN)]
    another operation x1 -> x0, local copies, waits for them, and re-layouts: 1.15 us -> none  [local(): strips = facet_strips[0, 0].reshape(2, COLS, CONTRIB, CONTRIB) * f32(window)]
    pallas_call x1, Pallas kernels: 48.9 us -> 49.8 us  [local(): pl.pallas_call(major_kernel, out_shape=jax.ShapeDtypeStruct((2, FN), jnp....]
    unnamed x10 -> x1, local copies, waits for them, and re-layouts: 1.3 us -> 1.38 us
where the time goes in v4:
time: 51.7 us; the launch traced here: 51.2 us
  Pallas kernels  49.8 us (96%)
  local copies, waits for them, and re-layouts  1.38 us (3%)
    pallas_call x1, Pallas kernels, local(): pl.pallas_call(major_kernel, out_shape=jax.ShapeDtypeStruct((2, FN), jnp....  49.8 us
    unnamed x1, local copies, waits for them, and re-layouts  1.38 us

profile of v4, /device:TPU:1, one launch (start us, length us, event | category | flops | bytes accessed | tf_op | source)
XLA Modules:
  0.0 51.2 jit_solution(13821863802406352210)
XLA Ops:
  0.0 49.8 %shard_map.109 = f32[2,4096]{1,0:T(2,128)} custom-call(f32[2,8,4096]{2,1,0:T(8,128)} %bitcast.6, s32[2,64]{1,0:T(2,128)} %offsets_ref.1, f32[5,128,128]{2,1,0:T(8,128)} %constant.10.clone.tables_ref, f32[256,64]{1,0:T(8,128)} %constant.11.clone.split_ref, f32[2,64,128]{2,1,0:T(8,128)} %constant.12.clone.turn_ref, f32[64,128]{1,0:T(8,128)} %constant.13.clone.window_ref, ...), custom_call_target="tpu_custom_call" | custom-call | tf_op jit(solution)/shard_map/pallas_call | solution.py:357
  49.8 1.4 %copy.13 = f32[1,1,2,4096]{3,2,1,0:T(2,128)} copy(f32[1,1,2,4096]{3,2,1,0:T(2,128)} %bitcast.7) | data formatting | bytes 65536

commit v5 on v4

--- a/solution.py
+++ b/solution.py
@@ -181,6 +181,18 @@
         part = ref.at[pl.ds(0, count)]
         pltpu.make_async_copy(part, part, sem).wait()
 
+    far = facets // 2
+
+    def send(t, to):
+        pltpu.make_async_remote_copy(
+            src_ref=leaving_ref.at[t, to],
+            dst_ref=arrived_ref.at[t, me],
+            send_sem=sems.at[t],
+            recv_sem=sems.at[2 + t],
+            device_id={"facet": to},
+            device_id_type=pl.DeviceIdType.MESH,
+        ).start()
+
     owns = []
     for t in range(FRONTS):
         own = pltpu.make_async_copy(
@@ -189,17 +201,13 @@
         own.start()
         owns.append(own)
 
-        @pl.loop(1, facets)
+        @pl.loop(0, far)
         def _(k):
-            to = lax.rem(me + 27 * k, facets)
-            pltpu.make_async_remote_copy(
-                src_ref=leaving_ref.at[t, to],
-                dst_ref=arrived_ref.at[t, me],
-                send_sem=sems.at[t],
-                recv_sem=sems.at[2 + t],
-                device_id={"facet": to},
-                device_id_type=pl.DeviceIdType.MESH,
-            ).start()
+            send(t, lax.rem(me // far + 1, 2) * far + lax.rem(me + 11 * k, far))
+
+        @pl.loop(1, far)
+        def _(k):
+            send(t, me // far * far + lax.rem(me + 11 * k, far))
 
     for t in range(FRONTS):
         col = cells_ref[t, 1:2, :]

time: 51.7 us -> 51.2 us (level)
  no operation moved by 1% of the time
where the time goes in v5:
time: 51.2 us; the launch traced here: 50.9 us
  Pallas kernels  49.5 us (97%)
  local copies, waits for them, and re-layouts  1.38 us (3%)
    pallas_call x1, Pallas kernels, local(): pl.pallas_call(major_kernel, out_shape=jax.ShapeDtypeStruct((2, FN), jnp....  49.5 us
    unnamed x1, local copies, waits for them, and re-layouts  1.38 us

profile of v5, /device:TPU:1, one launch (start us, length us, event | category | flops | bytes accessed | tf_op | source)
XLA Modules:
  0.0 50.9 jit_solution(16479770517346448360)
XLA Ops:
  0.0 49.5 %shard_map.109 = f32[2,4096]{1,0:T(2,128)} custom-call(f32[2,8,4096]{2,1,0:T(8,128)} %bitcast.6, s32[2,64]{1,0:T(2,128)} %offsets_ref.1, f32[5,128,128]{2,1,0:T(8,128)} %constant.10.clone.tables_ref, f32[256,64]{1,0:T(8,128)} %constant.11.clone.split_ref, f32[2,64,128]{2,1,0:T(8,128)} %constant.12.clone.turn_ref, f32[64,128]{1,0:T(8,128)} %constant.13.clone.window_ref, ...), custom_call_target="tpu_custom_call" | custom-call | tf_op jit(solution)/shard_map/pallas_call | solution.py:365
  49.5 1.4 %copy.13 = f32[1,1,2,4096]{3,2,1,0:T(2,128)} copy(f32[1,1,2,4096]{3,2,1,0:T(2,128)} %bitcast.7) | data formatting | bytes 65536
